TPU v7x, 512 devices: a whole 4x8x8 slice. The times are simulated.
512 devices in a mesh: expert: 32 (over z_lo, y, core), tensor: 16 (over z_hi, x).
Axes of the slice: x: 4, y: 8, z: 8 (z_hi: 4, z_lo: 2; z = z_hi * 2 + z_lo), core: 2. Of those that a mesh axis runs over, the one named last changes fastest.
Arguments:
- tokens: bfloat16 [4096, 4096], P('expert', 'tensor'), may hold values from -6 to 6
- routes: int32 [4096, 2], P('expert'), may hold values from 0 to 31, all different within a row; in each aligned block of 128 rows (0 to 127, 128 to 255, ...) at most 16 rows name the same one
- route_gates: float32 [4096, 2], P('expert'), may hold values from 0.1 to 0.6
- gate_weight: bfloat16 [32, 4096, 2048], P('expert', None, 'tensor'), may hold values from -0.09375 to 0.09375
- up_weight: bfloat16 [32, 4096, 2048], P('expert', None, 'tensor'), may hold values from -0.09375 to 0.09375
- down_weight: bfloat16 [32, 2048, 4096], P('expert', 'tensor'), may hold values from -0.1875 to 0.1875
Outputs:
- combined: bfloat16 [4096, 4096], P('expert', 'tensor')
Inputs may be any that keep to these rules, and one draw needn't show every extreme that they name: Within each aligned block of 128 tokens no expert is named by more than 16 routes, and the 2 experts of one token differ.
All inputs are finite; a program needn't handle non-finite values.
Results may differ from a plain program's by a relative error of at most 0.02.
Values may be sent and summed in bfloat16 or wider, within the bound.
A program may use at most 64 MiB of HBM per device.

v0:
```python
import jax
import jax.numpy as jnp
from jax import lax
from jax.sharding import PartitionSpec as P


def shards(tokens, routes, route_gates, gate_weight, up_weight, down_weight):
    token_count = tokens.shape[0]
    slice_width = tokens.shape[1]
    route_count = routes.shape[1]
    source_count = lax.axis_size("expert")
    expert_count = gate_weight.shape[0] * source_count
    capacity = 2 * token_count * route_count // expert_count
    slot_total = source_count * capacity
    flat_routes = routes.reshape(-1)
    onehot = (flat_routes[:, None] == jnp.arange(expert_count, dtype=jnp.int32)[None, :]).astype(
        jnp.int32
    )
    before = jnp.cumsum(onehot, axis=0) - onehot
    slot_ids = jnp.sum(before * onehot, axis=1)
    places = flat_routes * capacity + slot_ids
    token_ids = jnp.arange(token_count * route_count, dtype=jnp.int32) // route_count
    outgoing = (
        jnp.zeros((expert_count * capacity, slice_width), jnp.bfloat16)
        .at[places]
        .set(tokens[token_ids])
    )
    outgoing = outgoing.reshape(expert_count, capacity, slice_width)
    arrived = lax.all_to_all(outgoing, "expert", split_axis=0, concat_axis=0, tiled=True)
    received = arrived.reshape(slot_total, slice_width)
    gate_local = gate_weight[0]
    up_local = up_weight[0]
    down_local = down_weight[0]
    segment = lax.all_gather(received, "tensor", axis=1, tiled=True)
    gate_proj = jnp.dot(segment, gate_local, preferred_element_type=jnp.float32)
    up_proj = jnp.dot(segment, up_local, preferred_element_type=jnp.float32)
    hidden = (jax.nn.silu(gate_proj) * up_proj).astype(jnp.bfloat16)
    partial_value = lax.dot_general(
        down_local, hidden, (((0,), (1,)), ((), ())), preferred_element_type=jnp.float32
    )
    summed = lax.psum_scatter(
        partial_value.astype(jnp.bfloat16).astype(jnp.float32).astype(jnp.bfloat16),
        "tensor",
        scatter_dimension=0,
        tiled=True,
    )
    expert_out = summed.reshape(slice_width, source_count, capacity)
    returned = lax.all_to_all(expert_out, "expert", split_axis=1, concat_axis=1, tiled=True)
    flat_back = returned.reshape(slice_width, expert_count * capacity)
    picked = jnp.take(flat_back, places, axis=1).astype(jnp.float32)
    weighted = picked * route_gates.reshape(-1)[None, :]
    combined = jnp.sum(weighted.reshape(slice_width, token_count, route_count), axis=2)
    return combined.T.astype(jnp.bfloat16)


def solution(mesh):
    return jax.shard_map(
        shards,
        mesh=mesh,
        in_specs=(
            P("expert", "tensor"),
            P("expert", None),
            P("expert", None),
            P("expert", None, "tensor"),
            P("expert", None, "tensor"),
            P("expert", "tensor", None),
        ),
        out_specs=P("expert", "tensor"),
        check_vma=False,
    )
```

profile of v0, /device:TPU:1, one launch (start us, length us, event | category | flops | bytes accessed | tf_op | source)
XLA Modules:
  0.0 265.8 jit_solution(1499888292389562312)
XLA Ops:
  6.5 0.0 copy-start
  6.5 0.0 all-gather.2.cloned.1.call-start
  6.5 0.9 copy.14
  7.5 0.1 eq.26
  7.6 0.1 reshape.123
  7.8 0.7 broadcast_multiply_fusion
  8.5 0.6 reduce-window.6
  9.1 0.2 slice_reduce_fusion
  9.3 0.1 copy.19
  9.4 0.1 mul.41
  9.6 0.1 fusion.18
  9.7 3.6 %scatter_custom_fusion = bf16[512,256]{1,0:T(8,128)(2,1)S(1)} fusion(s32[256]{0:T(256)S(1)} %bitcast.52, bf16[128,256]{1,0:T(8,128)(2,1)} %param.6, s32[1024]{0:T(1024)S(1)} %pad_clamp_fusion.1, bf16[]{:T(256)} %constant.42.clone.1), kind=kCustom, calls=%fused_computation.18 | custom fusion | bytes 262656 | tf_op jit(solution)/shard_map/scatter | solution.py:26
  13.2 22.4 %all_to_all.10 = bf16[32,16,256]{2,1,0:T(8,128)(2,1)} all-to-all(bf16[32,16,256]{2,1,0:T(8,128)(2,1)S(1)} %bitcast.48), channel_id=1, replica_groups=mesh['expert'=32,'tensor'=16] {'expert'}, dimensions={0} | all-to-all | bytes 524288 | tf_op jit(solution)/shard_map/all_to_all | solution.py:29
  35.6 0.0 all-gather.2.cloned.1.call-update
  35.7 0.0 reduce-scatter.2.cloned.1.call-start
  35.7 88.7 %all-gather.2.cloned.1.call-done = bf16[512,4096]{1,0:T(8,128)(2,1)} async-done(((bf16[512,256]{1,0:T(8,128)(2,1)}), bf16[512,4096]{1,0:T(8,128)(2,1)}) %all-gather.2.cloned.1.call-update) | async-done | bytes 4194320 | tf_op jit(solution)/shard_map/all_gather | solution.py:34
  124.4 3.7 %fusion.5 = f32[512,128]{1,0:T(8,128)S(1)} fusion(bf16[512,4096]{1,0:T(8,128)(2,1)} %all-gather.2.cloned.1.call-done, bf16[1,4096,128]{2,1,0:T(8,128)(2,1)} %param.9), kind=kOutput, calls=%fused_computation.9 | convolution fusion | flops 536870912 | bytes 5505024 | tf_op jit(solution)/shard_map/dot_general | solution.py:35
  128.1 0.0 copy-done
  128.1 0.0 copy-done.1
  128.1 8.6 %fusion = bf16[4096,512]{0,1:T(8,128)(2,1)} fusion(bf16[512,4096]{1,0:T(8,128)(2,1)} %all-gather.2.cloned.1.call-done, bf16[1,128,4096]{2,1,0:T(8,128)(2,1)S(1)} %copy-done, bf16[1,4096,128]{2,1,0:T(8,128)(2,1)S(1)} %copy-done.1, f32[512,128]{1,0:T(8,128)S(1)} %fusion.5), kind=kOutput, calls=%fused_computation.4 | convolution fusion | flops 1076232192 | bytes 10747904 | tf_op jit(solution)/shard_map/dot_general | solution.py:38
  136.8 0.0 reduce-scatter.2.cloned.1.call-update
  136.8 98.8 %reduce-scatter.2.cloned.1.call-done = bf16[256,512]{0,1:T(8,128)(2,1)} async-done(((bf16[4096,512]{0,1:T(8,128)(2,1)}), bf16[256,512]{0,1:T(8,128)(2,1)}) %reduce-scatter.2.cloned.1.call-update) | async-done | bytes 262160 | tf_op jit(solution)/shard_map/reduce_scatter | solution.py:41
  235.5 8.5 %all-to-all-start.1 = ((bf16[256,32,16]{0,2,1:T(8,128)(2,1)}), bf16[256,32,16]{0,2,1:T(8,128)(2,1)S(1)}, u32[]{:S(2)}, u32[]{:S(2)}) async-start(bf16[256,32,16]{0,2,1:T(8,128)(2,1)} %bitcast.50), calls=%async_computation.2 | async-start | bytes 524288 | tf_op jit(solution)/shard_map/all_to_all | solution.py:48
  244.0 0.1 reduce_sum.23
  244.2 0.1 copy.17
  244.2 0.0 copy-done.2
  244.3 0.1 copy.18
  244.4 0.1 copy.20
  244.5 11.4 %all-to-all-done.1 = bf16[256,32,16]{0,2,1:T(8,128)(2,1)S(1)} async-done(((bf16[256,32,16]{0,2,1:T(8,128)(2,1)}), bf16[256,32,16]{0,2,1:T(8,128)(2,1)S(1)}, u32[]{:S(2)}, u32[]{:S(2)}) %all-to-all-start.1) | async-done | bytes 262176 | tf_op jit(solution)/shard_map/all_to_all | solution.py:48
  255.9 1.2 gather_fusion
  257.1 0.1 gather.11
  257.2 1.8 multiply_reduce_fusion
  (12 shorter events, 0.1 us)
Async XLA Ops:
  6.5 121.6 %copy-start = (bf16[1,128,4096]{2,1,0:T(8,128)(2,1)S(1)}, bf16[1,128,4096]{2,1,0:T(8,128)(2,1)}, u32[]{:S(2)}) copy-start(bf16[1,128,4096]{2,1,0:T(8,128)(2,1)} %param.11) | copy-start | bytes 3145732
  6.5 121.6 %copy-start.1 = (bf16[1,4096,128]{2,1,0:T(8,128)(2,1)S(1)}, bf16[1,4096,128]{2,1,0:T(8,128)(2,1)}, u32[]{:S(2)}) copy-start(bf16[1,4096,128]{2,1,0:T(8,128)(2,1)} %param.10) | copy-start | bytes 3145732
  6.5 117.8 %all-gather.2.cloned.1.call-start = ((), (), s32[]{:S(2)}) async-start(), calls=%async_computation.3 | async-start | bytes 4456448 | tf_op jit(solution)/shard_map/all_gather | solution.py:34
  35.7 199.9 %reduce-scatter.2.cloned.1.call-start = ((), (), s32[]{:S(2)}) async-start(), calls=%async_computation.4 | async-start | bytes 4456448 | tf_op jit(solution)/shard_map/reduce_scatter | solution.py:41
  136.8 107.5 %copy-start.2 = (s32[128,2]{0,1:T(2,128)S(1)}, s32[128,2]{0,1:T(2,128)}, u32[]{:S(2)}) copy-start(s32[128,2]{0,1:T(2,128)} %param.7) | copy-start | bytes 3076
  136.8 107.6 %copy-start.3 = (f32[128,2]{0,1:T(2,128)S(1)}, f32[128,2]{0,1:T(2,128)}, u32[]{:S(2)}) copy-start(f32[128,2]{0,1:T(2,128)} %param.8) | copy-start | bytes 3076
  235.5 20.4 %all-to-all-start.1 = ((bf16[256,32,16]{0,2,1:T(8,128)(2,1)}), bf16[256,32,16]{0,2,1:T(8,128)(2,1)S(1)}, u32[]{:S(2)}, u32[]{:S(2)}) async-start(bf16[256,32,16]{0,2,1:T(8,128)(2,1)} %bitcast.50), calls=%async_computation.2 | async-start | bytes 524288 | tf_op jit(solution)/shard_map/all_to_all | solution.py:48
Sparse Core Ops, SparseCore 0:
  35.8 88.5 all-gather.1
  136.9 98.5 reduce-scatter.1
where the time goes:
time: 266 us
  waiting for transfers between devices  199 us (75%)
  blocking collectives  22.4 us (8%)
  between operations  13.5 us (5%)
  matrix products  12.4 us (5%)
  starting transfers between devices  8.52 us (3%)
  local copies, waits for them, and re-layouts  6.89 us (3%)
  other arithmetic  3.28 us (1%)
    reduce_scatter x1, waiting for transfers between devices, shards(): lax.psum_scatter(partial_value.astype(jnp.bfloat16).astype(jnp.float32).a...  98.8 us
    all_gather x1, waiting for transfers between devices, shards(): segment = lax.all_gather(received, 'tensor', axis=1, tiled=True)  88.7 us
    all_to_all x1, blocking collectives, shards(): lax.all_to_all(outgoing, 'expert', split_axis=0, concat_axis=0, tiled=True)  22.4 us
    all_to_all x1, waiting for transfers between devices, shards(): lax.all_to_all(expert_out, 'expert', split_axis=1, concat_axis=1, tiled=T...  11.4 us
    dot_general x1, matrix products, shards(): lax.dot_general(down_local, hidden, (((0,), (1,)), ((), ())), preferred_e...  8.64 us
    all_to_all x1, starting transfers between devices, shards(): lax.all_to_all(expert_out, 'expert', split_axis=1, concat_axis=1, tiled=T...  8.48 us
  transfers between devices with their start and end apart: 3, of which 3 were waited for; matrix products, arithmetic and copies ran while one was open for 0% of the time, Pallas kernels for 0%

commit v1 on v0

v1 whole, which is shorter than its diff:
```python
import jax
import jax.numpy as jnp
from jax import lax
from jax.experimental import pallas as pl
from jax.experimental.pallas import tpu as pltpu
from jax.sharding import PartitionSpec as P

MESH = pl.DeviceIdType.MESH
F32, BF16 = jnp.float32, jnp.bfloat16
CHUNKS = 4
RING = 4


def remote(src, dst, send, recv, device):
    return pltpu.make_async_remote_copy(
        src_ref=src, dst_ref=dst, send_sem=send, recv_sem=recv, device_id=device, device_id_type=MESH
    )


def layer(
    tok, routes, gates, gate_hbm, up_hbm, down_hbm, out,
    outgoing, xs, ps, x_one, x_two, z_one, z_two, back, w_in, w_out,
    w_sem, a_send, a_recv, gz_send, gz_recv, gx_send, gx_recv,
    sx_send, sx_recv, sz_send, sz_recv, b_send, b_recv,
):
    e, t = lax.axis_index("expert"), lax.axis_index("tensor")
    core, y, zl = e % 2, (e // 2) % 8, e // 16
    x, zh = t % RING, t // RING
    x_up, x_far, x_dn = (x + 1) % RING, (x + 2) % RING, (x + 3) % RING
    z_up, z_far, z_dn = (zh + 1) % RING, (zh + 2) % RING, (zh + 3) % RING
    to_xu, to_xd = (e, zh * RING + x_up), (e, zh * RING + x_dn)
    to_zu, to_zd = (e, z_up * RING + x), (e, z_dn * RING + x)
    experts, cap = 32, 16
    tokens, width = tok.shape
    rows = xs.shape[3]
    half = rows // 2
    per = rows // cap

    def partner(j, sign):
        k, f = j // 4, j % 4
        dy = (k % 2) * ((k + 1) // 2) - (1 - k % 2) * (k // 2)
        return (((zl + f // 2) % 2) * 8 + (y + sign * dy + 8) % 8) * 2 + (core + f % 2) % 2

    def slot(i):
        return pl.ds(pl.multiple_of(i * cap, cap), cap)

    barrier = pltpu.get_barrier_semaphore()

    def greet(j, carry):
        pl.semaphore_signal(barrier, inc=1, device_id=(partner(j, 1), t), device_id_type=MESH)
        return carry

    lax.fori_loop(1, experts, greet, 0)
    for device in (to_xu, to_xd, to_zu, to_zd):
        pl.semaphore_signal(barrier, inc=1, device_id=device, device_id_type=MESH)

    hidden_block = gate_hbm.shape[1]
    loads = [
        pltpu.make_async_copy(gate_hbm, w_in.at[:, pl.ds(0, hidden_block)], w_sem.at[0]),
        pltpu.make_async_copy(up_hbm, w_in.at[:, pl.ds(hidden_block, hidden_block)], w_sem.at[1]),
        pltpu.make_async_copy(down_hbm, w_out, w_sem.at[2]),
    ]
    for load in loads:
        load.start()

    first, second = routes[0:1, :], routes[1:2, :]
    names = lax.broadcasted_iota(jnp.int32, (experts, tokens), 0)
    one, two = names == first, names == second
    count = (jnp.where(one, 1.0, 0.0) + jnp.where(two, 1.0, 0.0)).astype(BF16)
    earlier = lax.broadcasted_iota(jnp.int32, (tokens, tokens), 0) < lax.broadcasted_iota(
        jnp.int32, (tokens, tokens), 1
    )
    before = jnp.dot(count, jnp.where(earlier, 1.0, 0.0).astype(BF16), preferred_element_type=F32)
    place_one = first.astype(F32) * cap + jnp.sum(jnp.where(one, before, 0.0), axis=0, keepdims=True)
    place_two = second.astype(F32) * cap + jnp.sum(jnp.where(two, before, 0.0), axis=0, keepdims=True)
    places = lax.broadcasted_iota(jnp.int32, (experts * cap, tokens), 0).astype(F32)
    at_one, at_two = places == place_one, places == place_two
    picks = (jnp.where(at_one, 1.0, 0.0) + jnp.where(at_two, 1.0, 0.0)).astype(BF16)
    outgoing[...] = jnp.dot(picks, tok[...], preferred_element_type=F32).astype(BF16)

    pl.semaphore_wait(barrier, experts - 1 + 4)

    def dispatch(j, carry):
        d = partner(j, -1)
        remote(
            outgoing.at[slot(d)], xs.at[x, j // per, zh, slot(j % per)], a_send, a_recv.at[j], (d, t)
        ).start()
        return carry

    lax.fori_loop(1, experts, dispatch, 0)
    xs[x, 0, zh, pl.ds(0, cap), :] = outgoing[slot(e), :]
    for load in loads:
        load.wait()

    def arrived(ref, sem):
        remote(ref, ref, gz_send, sem, to_zu).wait_recv()

    def gather_z(c):
        def wait(j, carry):
            @pl.when(j > 0)
            def _():
                arrived(outgoing.at[slot(0)], a_recv.at[j])

            return carry

        lax.fori_loop(c * per, c * per + per, wait, 0)
        own = xs.at[x, c, zh]
        remote(own, own, gz_send, gz_recv.at[0, c], to_zu).start()
        remote(own, own, gz_send, gz_recv.at[1, c], to_zd).start()

    def forward_z(c):
        arrived(xs.at[x, c, z_dn], gz_recv.at[0, c])
        low = xs.at[x, c, z_dn, pl.ds(0, half)]
        remote(low, low, gz_send, gz_recv.at[2, c], to_zu).start()
        arrived(xs.at[x, c, z_up], gz_recv.at[1, c])
        high = xs.at[x, c, z_up, pl.ds(half, half)]
        remote(high, high, gz_send, gz_recv.at[3, c], to_zd).start()

    def gather_x(c):
        arrived(xs.at[x, c, z_far, pl.ds(0, half)], gz_recv.at[2, c])
        arrived(xs.at[x, c, z_far, pl.ds(half, half)], gz_recv.at[3, c])
        own = xs.at[x, c]
        remote(own, own, gx_send, gx_recv.at[0, c], to_xu).start()
        remote(own, own, gx_send, gx_recv.at[1, c], to_xd).start()

    def forward_x(c):
        arrived(xs.at[x_dn, c], gx_recv.at[0, c])
        low = xs.at[x_dn, c, pl.ds(0, 2)]
        remote(low, low, gx_send, gx_recv.at[2, c], to_xu).start()
        arrived(xs.at[x_up, c], gx_recv.at[1, c])
        high = xs.at[x_up, c, pl.ds(2, 2)]
        remote(high, high, gx_send, gx_recv.at[3, c], to_xd).start()

    def feed_forward(c):
        arrived(xs.at[x_far, c, pl.ds(0, 2)], gx_recv.at[2, c])
        arrived(xs.at[x_far, c, pl.ds(2, 2)], gx_recv.at[3, c])
        total = jnp.zeros((rows, 2 * hidden_block), F32)
        for block in range(RING * RING):
            total += jnp.dot(
                xs[block % RING, c, block // RING],
                w_in[block * width : (block + 1) * width, :],
                preferred_element_type=F32,
            )
        gate, up = total[:, :hidden_block], total[:, hidden_block:]
        hidden = (gate / (1.0 + jnp.exp(-gate)) * up).astype(BF16)
        for block in range(RING * RING):
            ps[block % RING, c, block // RING] = jnp.dot(
                hidden, w_out[:, block * width : (block + 1) * width], preferred_element_type=F32
            ).astype(BF16)
        remote(ps.at[x_far, c, pl.ds(0, 2)], x_one.at[0, c], sx_send, sx_recv.at[0, c], to_xu).start()
        remote(ps.at[x_far, c, pl.ds(2, 2)], x_one.at[1, c], sx_send, sx_recv.at[1, c], to_xd).start()
        remote(
            ps.at[x_up, c, pl.ds(2, 2)], x_two.at[0, c, pl.ds(2, 2)], sx_send, sx_recv.at[2, c], to_xu
        ).start()
        remote(
            ps.at[x_dn, c, pl.ds(0, 2)], x_two.at[1, c, pl.ds(0, 2)], sx_send, sx_recv.at[3, c], to_xd
        ).start()

    def add(*terms):
        return sum(term.astype(F32) for term in terms).astype(BF16)

    def relay_x(c):
        arrived(x_one.at[0, c], sx_recv.at[0, c])
        ps[x_up, c, 0:2] = add(ps[x_up, c, 0:2], x_one[0, c])
        remote(
            ps.at[x_up, c, pl.ds(0, 2)], x_two.at[0, c, pl.ds(0, 2)], sx_send, sx_recv.at[4, c], to_xu
        ).start()
        arrived(x_one.at[1, c], sx_recv.at[1, c])
        ps[x_dn, c, 2:4] = add(ps[x_dn, c, 2:4], x_one[1, c])
        remote(
            ps.at[x_dn, c, pl.ds(2, 2)], x_two.at[1, c, pl.ds(2, 2)], sx_send, sx_recv.at[5, c], to_xd
        ).start()

    def scatter_z(c):
        arrived(x_two.at[0, c, pl.ds(2, 2)], sx_recv.at[2, c])
        arrived(x_two.at[1, c, pl.ds(0, 2)], sx_recv.at[3, c])
        arrived(x_two.at[0, c, pl.ds(0, 2)], sx_recv.at[4, c])
        arrived(x_two.at[1, c, pl.ds(2, 2)], sx_recv.at[5, c])
        ps[x, c] = add(ps[x, c], x_two[0, c], x_two[1, c])
        low, high = pl.ds(0, half), pl.ds(half, half)
        remote(ps.at[x, c, z_far, low], z_one.at[0, c], sz_send, sz_recv.at[0, c], to_zu).start()
        remote(ps.at[x, c, z_far, high], z_one.at[1, c], sz_send, sz_recv.at[1, c], to_zd).start()
        remote(ps.at[x, c, z_up, high], z_two.at[0, c, high], sz_send, sz_recv.at[2, c], to_zu).start()
        remote(ps.at[x, c, z_dn, low], z_two.at[1, c, low], sz_send, sz_recv.at[3, c], to_zd).start()

    def relay_z(c):
        low, high = pl.ds(0, half), pl.ds(half, half)
        arrived(z_one.at[0, c], sz_recv.at[0, c])
        ps[x, c, z_up, 0:half] = add(ps[x, c, z_up, 0:half], z_one[0, c])
        remote(ps.at[x, c, z_up, low], z_two.at[0, c, low], sz_send, sz_recv.at[4, c], to_zu).start()
        arrived(z_one.at[1, c], sz_recv.at[1, c])
        ps[x, c, z_dn, half:rows] = add(ps[x, c, z_dn, half:rows], z_one[1, c])
        remote(ps.at[x, c, z_dn, high], z_two.at[1, c, high], sz_send, sz_recv.at[5, c], to_zd).start()

    def give_back(c):
        low, high = pl.ds(0, half), pl.ds(half, half)
        arrived(z_two.at[0, c, high], sz_recv.at[2, c])
        arrived(z_two.at[1, c, low], sz_recv.at[3, c])
        arrived(z_two.at[0, c, low], sz_recv.at[4, c])
        arrived(z_two.at[1, c, high], sz_recv.at[5, c])
        ps[x, c, zh] = add(ps[x, c, zh], z_two[0, c], z_two[1, c])

        def send(i, carry):
            j = c * per + i

            @pl.when(j > 0)
            def _():
                remote(
                    ps.at[x, c, zh, slot(i)], back.at[slot(e)], b_send, b_recv.at[e], (partner(j, 1), t)
                ).start()

            return carry

        lax.fori_loop(0, per, send, 0)

    stages = (
        gather_z, forward_z, gather_x, forward_x, feed_forward, relay_x, scatter_z, relay_z, give_back
    )

    def tick(s, carry):
        for number, stage in enumerate(stages):
            c = s - number

            @pl.when((c >= 0) & (c < CHUNKS))
            def _(stage=stage, c=c):
                stage(c)

        return carry

    lax.fori_loop(0, CHUNKS + len(stages) - 1, tick, 0)

    back[slot(e), :] = ps[x, 0, zh, pl.ds(0, cap), :]

    def collect(j, carry):
        @pl.when(j != e)
        def _():
            arrived(back.at[slot(0)], b_recv.at[j])

        return carry

    lax.fori_loop(0, experts, collect, 0)
    share = jnp.where(at_one, gates[0:1, :], 0.0) + jnp.where(at_two, gates[1:2, :], 0.0)
    coarse = share.astype(BF16)
    fine = (share - coarse.astype(F32)).astype(BF16)
    contract = (((0,), (0,)), ((), ()))
    returned = back[...]
    combined = lax.dot_general(coarse, returned, contract, preferred_element_type=F32)
    combined += lax.dot_general(fine, returned, contract, preferred_element_type=F32)
    out[...] = combined.astype(BF16)

    def sent(ref, sem):
        remote(ref, ref, sem, sz_recv.at[0, 0], to_zu).wait_send()

    most = pl.ds(0, (experts - 1) * cap)
    sent(outgoing.at[most], a_send)
    sent(back.at[most], b_send)
    sent(xs.at[0, pl.ds(0, 3)] if CHUNKS == 4 else xs.at[0, :, pl.ds(0, 3)], gz_send)
    sent(xs.at[pl.ds(0, 3)], gx_send)
    sent(ps.at[pl.ds(0, 3)], sx_send)
    sent(ps.at[0, pl.ds(0, 3)] if CHUNKS == 4 else ps.at[0, :, pl.ds(0, 3)], sz_send)


def shards(tokens, routes, route_gates, gate_weight, up_weight, down_weight):
    token_count, width = tokens.shape
    depth, block = gate_weight.shape[1:]
    experts, cap = 32, 16
    rows = experts * cap // CHUNKS
    dma, vmem = pltpu.SemaphoreType.DMA, pltpu.VMEM
    whole, left = pl.BlockSpec(memory_space=vmem), pl.BlockSpec(memory_space=pl.ANY)
    return pl.pallas_call(
        layer,
        out_shape=jax.ShapeDtypeStruct((token_count, width), BF16),
        in_specs=[whole, whole, whole, left, left, left],
        out_specs=whole,
        scratch_shapes=[
            vmem((experts * cap, width), BF16),
            vmem((RING, CHUNKS, RING, rows, width), BF16),
            vmem((RING, CHUNKS, RING, rows, width), BF16),
            vmem((2, CHUNKS, 2, rows, width), BF16),
            vmem((2, CHUNKS, RING, rows, width), BF16),
            vmem((2, CHUNKS, rows // 2, width), BF16),
            vmem((2, CHUNKS, rows, width), BF16),
            vmem((experts * cap, width), BF16),
            vmem((depth, 2 * block), BF16),
            vmem((block, depth), BF16),
            dma((3,)),
            dma,
            dma((experts,)),
            dma,
            dma((4, CHUNKS)),
            dma,
            dma((4, CHUNKS)),
            dma,
            dma((6, CHUNKS)),
            dma,
            dma((6, CHUNKS)),
            dma,
            dma((experts,)),
        ],
        compiler_params=pltpu.CompilerParams(
            collective_id=0, has_side_effects=True, vmem_limit_bytes=40 * 1024 * 1024
        ),
    )(tokens, routes.T, route_gates.T, gate_weight[0], up_weight[0], down_weight[0])


def solution(mesh):
    return jax.shard_map(
        shards,
        mesh=mesh,
        in_specs=(
            P("expert", "tensor"),
            P("expert", None),
            P("expert", None),
            P("expert", None, "tensor"),
            P("expert", None, "tensor"),
            P("expert", "tensor", None),
        ),
        out_specs=P("expert", "tensor"),
        check_vma=False,
    )
```

time: 266 us -> 128 us (0.48)
  waiting for transfers between devices: 199 us -> 0 us
  Pallas kernels: 0 us -> 120 us
  blocking collectives: 22.4 us -> 0 us
  between operations: 13.5 us -> 0.02 us
  matrix products: 12.4 us -> 0 us
  starting transfers between devices: 8.52 us -> 0 us
  other arithmetic: 3.28 us -> 0 us
    pallas_call x0 -> x1, Pallas kernels: none -> 120 us  [shards(): pl.pallas_call(layer, out_shape=jax.ShapeDtypeStruct((token_count, width)...]
    reduce_scatter x1 -> x0, waiting for transfers between devices: 98.8 us -> none  [shards(): lax.psum_scatter(partial_value.astype(jnp.bfloat16).astype(jnp.float32).a...]
    all_gather x1 -> x0, waiting for transfers between devices: 88.7 us -> none  [shards(): segment = lax.all_gather(received, 'tensor', axis=1, tiled=True)]
    all_to_all x1 -> x0, blocking collectives: 22.4 us -> none  [shards(): lax.all_to_all(outgoing, 'expert', split_axis=0, concat_axis=0, tiled=True)]
    dot_general x2 -> x0, matrix products: 12.4 us -> none  [the longest x1 8.64 us: shards(): lax.dot_general(down_local, hidden, (((0,), (1,)), ((), ())), preferred_e...]
    all_to_all x1 -> x0, waiting for transfers between devices: 11.4 us -> none  [shards(): lax.all_to_all(expert_out, 'expert', split_axis=1, concat_axis=1, tiled=T...]
    all_to_all x1 -> x0, starting transfers between devices: 8.48 us -> none  [shards(): lax.all_to_all(expert_out, 'expert', split_axis=1, concat_axis=1, tiled=T...]
    unnamed x10 -> x13, local copies, waits for them, and re-layouts: 1.06 us -> 5.84 us
  transfers between devices with their start and end apart: 3 -> 0, of which waited for: 3 -> 0; matrix products, arithmetic and copies ran while one was open for 0% -> 0% of each run, Pallas kernels for 0% -> 0%
where the time goes in v1:
time: 128 us; the launch traced here: 126 us
  Pallas kernels  120 us (94%)
  local copies, waits for them, and re-layouts  5.84 us (5%)
    pallas_call x1, Pallas kernels, shards(): pl.pallas_call(layer, out_shape=jax.ShapeDtypeStruct((token_count, width)...  120 us
    unnamed x13, local copies, waits for them, and re-layouts  5.84 us

profile of v1, /device:TPU:1, one launch (start us, length us, event | category | flops | bytes accessed | tf_op | source)
XLA Modules:
  0.0 125.7 jit_solution(13994940607278148311)
XLA Ops:
  0.0 0.0 copy-start.5
  0.0 0.0 copy-start.4
  0.0 0.7 copy-done.5
  0.7 0.0 copy-done.4
  0.7 0.0 copy-start
  0.7 1.2 copy-done
  1.9 0.0 copy-start.1
  1.9 1.2 copy-done.1
  3.1 0.0 copy-start.2
  3.1 1.2 copy-done.2
  4.4 0.0 copy-start.3
  4.4 0.8 copy-done.3
  5.2 119.9 %shard_map.64 = bf16[128,256]{1,0:T(8,128)(2,1)S(1)} custom-call(bf16[128,256]{1,0:T(8,128)(2,1)S(1)} %copy-done.3, s32[2,128]{1,0:T(2,128)S(1)} %bitcast.8, f32[2,128]{1,0:T(2,128)S(1)} %bitcast.9, bf16[4096,128]{1,0:T(8,128)(2,1)S(1)} %bitcast.5, bf16[4096,128]{1,0:T(8,128)(2,1)S(1)} %bitcast.6, bf16[128,4096]{1,0:T(8,128)(2,1)S(1)} %bitcast.7), custom_call_target="tpu_custom_call" | custom-call | tf_op jit(solution)/shard_map/pallas_call | solution.py:270
  125.1 0.6 copy.8
Async XLA Ops:
  0.0 0.7 copy-start.5
  0.0 0.7 copy-start.4
  0.7 1.2 copy-start
  1.9 1.2 copy-start.1
  3.1 1.2 copy-start.2
  4.4 0.8 copy-start.3

commit v2 on v0

v2 whole, which is shorter than its diff:
```python
import jax
import jax.numpy as jnp
from jax import lax
from jax.experimental import pallas as pl
from jax.experimental.pallas import tpu as pltpu
from jax.sharding import PartitionSpec as P

MESH = pl.DeviceIdType.MESH
F32, BF16 = jnp.float32, jnp.bfloat16
RING = 4
EXPERTS, CAP, CHUNKS = 32, 16, 4
PER = EXPERTS // CHUNKS
ROWS = PER * CAP
HOME = EXPERTS - 4


def remote(src, dst, send, recv, device):
    return pltpu.make_async_remote_copy(
        src_ref=src, dst_ref=dst, send_sem=send, recv_sem=recv, device_id=device, device_id_type=MESH
    )


def arrived(ref, sem, device):
    remote(ref, ref, sem, sem, device).wait_recv()


def sent(ref, sem, device):
    remote(ref, ref, sem, sem, device).wait_send()


def layer(
    tok_hbm, routes_hbm, gates_hbm, gate_hbm, up_hbm, down_hbm, out,
    tz, routes, gates, outgoing, xs, w_in, w_in_relay, w_out, w_out_relay,
    gu_out, gu_own, gu_in, hs, ps, back, share, cz, zr,
    l_sem, t_send, t_recv, wi_send, wi_recv, wo_send, wo_recv, a_send, a_recv,
    g_send, g_recv, h_send, h_recv, b_send, b_recv, z_send, z_recv,
):
    e, t = lax.axis_index("expert"), lax.axis_index("tensor")
    core, y, zl = e % 2, (e // 2) % 8, e // 16
    x, zh = t % RING, t // RING
    x_up, x_dn = (x + 1) % RING, (x + 3) % RING
    xu, xd = (e, zh * RING + x_up), (e, zh * RING + x_dn)
    tokens, width = out.shape
    block = w_in.shape[-1]

    def over_x(k):
        return (e, zh * RING + (x + k) % RING)

    def over_z(k):
        return (e, ((zh + k) % RING) * RING + x)

    def partner(j, sign):
        k, f = 7 - j // 4, j % 4
        dy = (k % 2) * ((k + 1) // 2) - (1 - k % 2) * (k // 2)
        return (((zl + f // 2) % 2) * 8 + (y + sign * dy + 8) % 8) * 2 + (core + f % 2) % 2

    barrier = pltpu.get_barrier_semaphore()

    def greet(j, carry):
        @pl.when(j != HOME)
        def _():
            pl.semaphore_signal(barrier, inc=1, device_id=(partner(j, 1), t), device_id_type=MESH)

        return carry

    for k in (1, 2, 3):
        pl.semaphore_signal(barrier, inc=1, device_id=over_z(k), device_id_type=MESH)
        pl.semaphore_signal(barrier, inc=1, device_id=over_x(k), device_id_type=MESH)
    lax.fori_loop(0, EXPERTS, greet, 0)

    smalls = [
        pltpu.make_async_copy(tok_hbm, tz.at[zh], l_sem.at[0]),
        pltpu.make_async_copy(routes_hbm, routes, l_sem.at[1]),
        pltpu.make_async_copy(gates_hbm, gates, l_sem.at[2]),
    ]
    mine = pl.ds(pl.multiple_of(x * block, block), block)
    loads_in = [
        pltpu.make_async_copy(gate_hbm.at[:, x], w_in.at[0, x], l_sem.at[3]),
        pltpu.make_async_copy(up_hbm.at[:, x], w_in.at[1, x], l_sem.at[4]),
    ]

    def columns(b, n):
        return pl.ds(pl.multiple_of((b * RING + n) * width, width), width)

    loads_out = [
        pltpu.make_async_copy(down_hbm.at[:, columns(b, x)], w_out.at[b, mine], l_sem.at[5 + b])
        for b in range(RING)
    ]
    for load in smalls:
        load.start()
    for load in smalls:
        load.wait()
    pl.semaphore_wait(barrier, EXPERTS - 1 + 6)

    for k in (2, 1, 3):
        remote(tz.at[zh], tz.at[zh], t_send, t_recv.at[k], over_z(k)).start()
    x_far = (x + 2) % RING
    remote(gate_hbm.at[:, x_far], w_in_relay.at[0], wi_send, wi_recv.at[0], xu).start()
    remote(up_hbm.at[:, x_far], w_in_relay.at[1], wi_send, wi_recv.at[1], xd).start()
    remote(gate_hbm.at[:, x_up], w_in.at[0, x], wi_send, wi_recv.at[2], xu).start()
    remote(gate_hbm.at[:, x_dn], w_in.at[0, x], wi_send, wi_recv.at[3], xd).start()
    remote(up_hbm.at[:, x_up], w_in.at[1, x], wi_send, wi_recv.at[4], xu).start()
    remote(up_hbm.at[:, x_dn], w_in.at[1, x], wi_send, wi_recv.at[5], xd).start()
    for load in loads_in + loads_out:
        load.start()

    first, second = routes[0:1, :], routes[1:2, :]
    names = lax.broadcasted_iota(jnp.int32, (EXPERTS, tokens), 0)
    one, two = names == first, names == second
    count = (jnp.where(one, 1.0, 0.0) + jnp.where(two, 1.0, 0.0)).astype(BF16)
    earlier = lax.broadcasted_iota(jnp.int32, (tokens, tokens), 0) < lax.broadcasted_iota(
        jnp.int32, (tokens, tokens), 1
    )
    before = jnp.dot(count, jnp.where(earlier, 1.0, 0.0).astype(BF16), preferred_element_type=F32)
    place_one = first.astype(F32) * CAP + jnp.sum(jnp.where(one, before, 0.0), axis=0, keepdims=True)
    place_two = second.astype(F32) * CAP + jnp.sum(jnp.where(two, before, 0.0), axis=0, keepdims=True)
    places = lax.broadcasted_iota(jnp.int32, (EXPERTS * CAP, tokens), 0).astype(F32)
    at_one, at_two = places == place_one, places == place_two
    picks = (jnp.where(at_one, 1.0, 0.0) + jnp.where(at_two, 1.0, 0.0)).astype(BF16)

    for k in (0, 1, 3, 2):
        n = (zh + 4 - k) % RING
        if k:
            arrived(tz.at[n], t_recv.at[k], over_z(1))
        picked = jnp.dot(picks, tz[n], preferred_element_type=F32).astype(BF16)
        outgoing[:, n] = picked.reshape(EXPERTS, CAP, width)

    def dispatch(j, carry):
        @pl.when(j != HOME)
        def _():
            d = partner(j, -1)
            remote(outgoing.at[d], xs.at[j // PER, j % PER], a_send, a_recv.at[j], (d, t)).start()

        return carry

    lax.fori_loop(0, EXPERTS, dispatch, 0)
    xs[HOME // PER, HOME % PER] = outgoing[e]

    arrived(w_in_relay.at[0], wi_recv.at[0], xu)
    remote(w_in_relay.at[0], w_in.at[0, x_dn], wi_send, wi_recv.at[6], xu).start()
    arrived(w_in_relay.at[1], wi_recv.at[1], xu)
    remote(w_in_relay.at[1], w_in.at[1, x_up], wi_send, wi_recv.at[7], xd).start()
    for b in (0, 1):
        remote(down_hbm.at[:, columns(b, x_far)], w_out_relay.at[0, b], wo_send, wo_recv.at[0], xu).start()
        remote(
            down_hbm.at[:, columns(b + 2, x_far)], w_out_relay.at[1, b], wo_send, wo_recv.at[1], xd
        ).start()
    for b in range(RING):
        remote(down_hbm.at[:, columns(b, x_up)], w_out.at[b, mine], wo_send, wo_recv.at[2], xu).start()
        remote(down_hbm.at[:, columns(b, x_dn)], w_out.at[b, mine], wo_send, wo_recv.at[3], xd).start()

    shared = jnp.where(at_one, gates[0:1, :], 0.0) + jnp.where(at_two, gates[1:2, :], 0.0)
    shared = shared.T
    coarse = shared.astype(BF16)
    share[0:tokens, :] = coarse
    share[tokens : 2 * tokens, :] = (shared - coarse.astype(F32)).astype(BF16)

    from_dn = pl.ds(pl.multiple_of(x_dn * block, block), block)
    from_up = pl.ds(pl.multiple_of(x_up * block, block), block)
    from_far = pl.ds(pl.multiple_of(x_far * block, block), block)

    for load in loads_in:
        load.wait()
    arrived(w_in.at[0, x_dn], wi_recv.at[2], xu)
    arrived(w_in.at[0, x_up], wi_recv.at[3], xu)
    arrived(w_in.at[1, x_dn], wi_recv.at[4], xu)
    arrived(w_in.at[1, x_up], wi_recv.at[5], xu)
    arrived(w_in.at[0, x_far], wi_recv.at[6], xu)
    arrived(w_in.at[1, x_far], wi_recv.at[7], xu)

    def project(c):
        def wait(i, carry):
            j = c * PER + i

            @pl.when(j != HOME)
            def _():
                arrived(xs.at[0, 0], a_recv.at[j], xu)

            return carry

        lax.fori_loop(0, PER, wait, 0)
        for k in (2, 1, 3, 0):
            n = (x + k) % RING
            total = jnp.zeros((ROWS, 2 * block), F32)
            for b in range(RING):
                weights = jnp.concatenate([w_in[0, n, b], w_in[1, n, b]], axis=1)
                total += jnp.dot(xs[c, :, b].reshape(ROWS, width), weights, preferred_element_type=F32)
            if k:
                gu_out[n, c] = total.astype(BF16)
                remote(gu_out.at[n, c], gu_in.at[k - 1, c], g_send, g_recv.at[k - 1, c], over_x(k)).start()
            else:
                gu_own[c] = total

    def activate(c):
        total = gu_own[c]
        for k in (1, 3, 2):
            arrived(gu_in.at[k - 1, c], g_recv.at[k - 1, c], xu)
            total += gu_in[k - 1, c].astype(F32)
        gate, up = total[:, :block], total[:, block:]
        hs[x, c] = (gate / (1.0 + jnp.exp(-gate)) * up).astype(BF16)
        for k in (2, 1, 3):
            remote(hs.at[x, c], hs.at[x, c], h_send, h_recv.at[k - 1, c], over_x(k)).start()

    def hand_on():
        arrived(w_out_relay.at[0], wo_recv.at[0], xu)
        low, high = pl.ds(0, 2), pl.ds(2, 2)
        remote(w_out_relay.at[0], w_out.at[low, from_dn], wo_send, wo_recv.at[4], xu).start()
        arrived(w_out_relay.at[1], wo_recv.at[1], xu)
        remote(w_out_relay.at[1], w_out.at[high, from_up], wo_send, wo_recv.at[5], xd).start()

    def have_out():
        for load in loads_out:
            load.wait()
        low, high = pl.ds(0, 2), pl.ds(2, 2)
        arrived(w_out.at[:, from_dn], wo_recv.at[2], xu)
        arrived(w_out.at[:, from_up], wo_recv.at[3], xu)
        arrived(w_out.at[low, from_far], wo_recv.at[4], xu)
        arrived(w_out.at[high, from_far], wo_recv.at[5], xu)

    def expand(c):
        for k in (1, 3, 2):
            n = (x + 4 - k) % RING
            arrived(hs.at[n, c], h_recv.at[k - 1, c], xu)
        hidden = jnp.concatenate([hs[n, c] for n in range(RING)], axis=1)
        for b in range(RING):
            part = jnp.dot(hidden, w_out[b], preferred_element_type=F32).astype(BF16)
            ps[c, :, b] = part.reshape(PER, CAP, width)

        def send(i, carry):
            j = c * PER + i

            @pl.when(j != HOME)
            def _():
                remote(ps.at[c, i], back.at[e], b_send, b_recv.at[e], (partner(j, 1), t)).start()

            return carry

        lax.fori_loop(0, PER, send, 0)

    def tick(s, carry):
        @pl.when(s < CHUNKS)
        def _():
            project(s)

        pl.when(s == 1)(hand_on)

        @pl.when((s >= 1) & (s <= CHUNKS))
        def _():
            activate(s - 1)

        pl.when(s == 2)(have_out)

        @pl.when(s >= 2)
        def _():
            expand(s - 2)

        return carry

    lax.fori_loop(0, CHUNKS + 2, tick, 0)
    back[e] = ps[HOME // PER, HOME % PER]

    def collect(j, carry):
        @pl.when(j != e)
        def _():
            arrived(back.at[0], b_recv.at[j], xu)

        return carry

    lax.fori_loop(0, EXPERTS, collect, 0)

    def combine(n):
        returned = back[:, n].reshape(EXPERTS * CAP, width)
        both = jnp.dot(share[...], returned, preferred_element_type=F32)
        return both[:tokens] + both[tokens:]

    for k in (2, 1, 3):
        n = (zh + k) % RING
        cz[n] = combine(n).astype(BF16)
        remote(cz.at[n], zr.at[k - 1], z_send, z_recv.at[k - 1], over_z(k)).start()
    total = combine(zh)
    for k in (1, 3, 2):
        arrived(zr.at[k - 1], z_recv.at[k - 1], xu)
        total += zr[k - 1].astype(F32)
    out[...] = total.astype(BF16)

    sent(tz.at[pl.ds(0, 3)], t_send, xu)
    sent(w_in, wi_send, xu)
    sent(w_out, wo_send, xu)
    sent(outgoing.at[pl.ds(0, EXPERTS - 1)], a_send, xu)
    sent(gu_out.at[pl.ds(0, 3)], g_send, xu)
    sent(hs.at[pl.ds(0, 3)], h_send, xu)
    sent(back.at[pl.ds(0, EXPERTS - 1)], b_send, xu)
    sent(cz.at[pl.ds(0, 3)], z_send, xu)


def shards(tokens, routes, route_gates, gate_weight, up_weight, down_weight):
    token_count, width = tokens.shape
    depth, block = gate_weight.shape[1:]
    dma, vmem = pltpu.SemaphoreType.DMA, pltpu.VMEM
    halves = (RING, RING, width, block)
    return pl.pallas_call(
        layer,
        out_shape=jax.ShapeDtypeStruct((token_count, width), BF16),
        in_specs=[pl.BlockSpec(memory_space=pltpu.HBM)] * 6,
        out_specs=pl.BlockSpec(memory_space=vmem),
        scratch_shapes=[
            vmem((RING, token_count, width), BF16),
            vmem((2, token_count), jnp.int32),
            vmem((2, token_count), F32),
            vmem((EXPERTS, RING, CAP, width), BF16),
            vmem((CHUNKS, PER, RING, CAP, width), BF16),
            vmem((2,) + halves, BF16),
            vmem((2,) + halves[1:], BF16),
            vmem((RING, RING * block, width), BF16),
            vmem((2, 2, block, width), BF16),
            vmem((RING, CHUNKS, ROWS, 2 * block), BF16),
            vmem((CHUNKS, ROWS, 2 * block), F32),
            vmem((RING - 1, CHUNKS, ROWS, 2 * block), BF16),
            vmem((RING, CHUNKS, ROWS, block), BF16),
            vmem((CHUNKS, PER, RING, CAP, width), BF16),
            vmem((EXPERTS, RING, CAP, width), BF16),
            vmem((2 * token_count, EXPERTS * CAP), BF16),
            vmem((RING, token_count, width), BF16),
            vmem((RING - 1, token_count, width), BF16),
            dma((5 + RING,)),
            dma,
            dma((RING,)),
            dma,
            dma((8,)),
            dma,
            dma((6,)),
            dma,
            dma((EXPERTS,)),
            dma,
            dma((RING - 1, CHUNKS)),
            dma,
            dma((RING - 1, CHUNKS)),
            dma,
            dma((EXPERTS,)),
            dma,
            dma((RING - 1,)),
        ],
        compiler_params=pltpu.CompilerParams(
            collective_id=0, has_side_effects=True, vmem_limit_bytes=62 * 1024 * 1024
        ),
    )(
        tokens,
        routes.T,
        route_gates.T,
        gate_weight.reshape(halves),
        up_weight.reshape(halves),
        down_weight[0],
    )


def solution(mesh):
    return jax.shard_map(
        shards,
        mesh=mesh,
        in_specs=(
            P("expert", "tensor"),
            P("expert", None),
            P("expert", None),
            P("expert", None, "tensor"),
            P("expert", None, "tensor"),
            P("expert", "tensor", None),
        ),
        out_specs=P("expert", "tensor"),
        check_vma=False,
    )
```

time: 266 us -> 97.4 us (0.37)
  waiting for transfers between devices: 199 us -> 0 us
  Pallas kernels: 0 us -> 95.7 us
  blocking collectives: 22.4 us -> 0 us
  between operations: 13.5 us -> 0.01 us
  matrix products: 12.4 us -> 0 us
  starting transfers between devices: 8.52 us -> 0 us
  local copies, waits for them, and re-layouts: 6.89 us -> 1.47 us
  other arithmetic: 3.28 us -> 0 us
    reduce_scatter x1 -> x0, waiting for transfers between devices: 98.8 us -> none  [shards(): lax.psum_scatter(partial_value.astype(jnp.bfloat16).astype(jnp.float32).a...]
    pallas_call x0 -> x1, Pallas kernels: none -> 95.7 us  [shards(): pl.pallas_call(layer, out_shape=jax.ShapeDtypeStruct((token_count, width)...]
    all_gather x1 -> x0, waiting for transfers between devices: 88.7 us -> none  [shards(): segment = lax.all_gather(received, 'tensor', axis=1, tiled=True)]
    all_to_all x1 -> x0, blocking collectives: 22.4 us -> none  [shards(): lax.all_to_all(outgoing, 'expert', split_axis=0, concat_axis=0, tiled=True)]
    dot_general x2 -> x0, matrix products: 12.4 us -> none  [the longest x1 8.64 us: shards(): lax.dot_general(down_local, hidden, (((0,), (1,)), ((), ())), preferred_e...]
    all_to_all x1 -> x0, waiting for transfers between devices: 11.4 us -> none  [shards(): lax.all_to_all(expert_out, 'expert', split_axis=1, concat_axis=1, tiled=T...]
    all_to_all x1 -> x0, starting transfers between devices: 8.48 us -> none  [shards(): lax.all_to_all(expert_out, 'expert', split_axis=1, concat_axis=1, tiled=T...]
    scatter x1 -> x0, local copies, waits for them, and re-layouts: 3.57 us -> none  [shards(): outgoing = jnp.zeros((expert_count * capacity, slice_width), jnp.bfloat16...]
  transfers between devices with their start and end apart: 3 -> 0, of which waited for: 3 -> 0; matrix products, arithmetic and copies ran while one was open for 0% -> 0% of each run, Pallas kernels for 0% -> 0%
where the time goes in v2:
time: 97.4 us; the launch traced here: 97.2 us
  Pallas kernels  95.7 us (98%)
  local copies, waits for them, and re-layouts  1.47 us (2%)
    pallas_call x1, Pallas kernels, shards(): pl.pallas_call(layer, out_shape=jax.ShapeDtypeStruct((token_count, width)...  95.7 us

profile of v2, /device:TPU:1, one launch (start us, length us, event | category | flops | bytes accessed | tf_op | source)
XLA Modules:
  0.0 97.2 jit_solution(6857056850242991343)
XLA Ops:
  0.0 95.7 %shard_map.64 = bf16[128,256]{1,0:T(8,128)(2,1)} custom-call(bf16[128,256]{1,0:T(8,128)(2,1)} %tok_hbm.1, s32[2,128]{1,0:T(2,128)} %bitcast.8, f32[2,128]{1,0:T(2,128)} %bitcast.9, bf16[4,4,256,128]{3,2,1,0:T(8,128)(2,1)} %bitcast.5, bf16[4,4,256,128]{3,2,1,0:T(8,128)(2,1)} %bitcast.6, bf16[128,4096]{1,0:T(8,128)(2,1)} %bitcast.7), custom_call_target="tpu_custom_call" | custom-call | tf_op jit(solution)/shard_map/pallas_call | solution.py:301
  95.7 1.5 %copy.8 = bf16[128,256]{1,0:T(8,128)(2,1)} copy(bf16[128,256]{1,0:T(8,128)(2,1)} %shard_map.64) | data formatting | bytes 131072

commit v3 on v2

--- a/solution.py
+++ b/solution.py
@@ -12,6 +12,8 @@
 PER = EXPERTS // CHUNKS
 ROWS = PER * CAP
 HOME = EXPERTS - 4
+FAR = EXPERTS // 2
+FAR_CHUNKS = CHUNKS // 2
 
 
 def remote(src, dst, send, recv, device):
@@ -30,10 +32,10 @@
 
 def layer(
     tok_hbm, routes_hbm, gates_hbm, gate_hbm, up_hbm, down_hbm, out,
-    tz, routes, gates, outgoing, xs, w_in, w_in_relay, w_out, w_out_relay,
-    gu_out, gu_own, gu_in, hs, ps, back, share, cz, zr,
-    l_sem, t_send, t_recv, wi_send, wi_recv, wo_send, wo_recv, a_send, a_recv,
-    g_send, g_recv, h_send, h_recv, b_send, b_recv, z_send, z_recv,
+    tz, routes, gates, out_far, out_near, xs, w_in, w_in_relay, w_out, w_out_relay,
+    gu_out, gu_own, gu_in, hs, ps, zs, sums, back_far, back_near, share, cz, zr,
+    l_sem, t_send, t_recv, wi_send, wi_recv, wo_send, wo_recv, f_send, a_send, a_recv, q_send, q_recv,
+    g_send, g_recv, h_send, h_recv, r_send, r_recv, s_send, b_send, b_recv, z_send, z_recv,
 ):
     e, t = lax.axis_index("expert"), lax.axis_index("tensor")
     core, y, zl = e % 2, (e // 2) % 8, e // 16
@@ -99,10 +101,6 @@
     remote(up_hbm.at[:, x_far], w_in_relay.at[1], wi_send, wi_recv.at[1], xd).start()
     remote(gate_hbm.at[:, x_up], w_in.at[0, x], wi_send, wi_recv.at[2], xu).start()
     remote(gate_hbm.at[:, x_dn], w_in.at[0, x], wi_send, wi_recv.at[3], xd).start()
-    remote(up_hbm.at[:, x_up], w_in.at[1, x], wi_send, wi_recv.at[4], xu).start()
-    remote(up_hbm.at[:, x_dn], w_in.at[1, x], wi_send, wi_recv.at[5], xd).start()
-    for load in loads_in + loads_out:
-        load.start()
 
     first, second = routes[0:1, :], routes[1:2, :]
     names = lax.broadcasted_iota(jnp.int32, (EXPERTS, tokens), 0)
@@ -112,34 +110,69 @@
         jnp.int32, (tokens, tokens), 1
     )
     before = jnp.dot(count, jnp.where(earlier, 1.0, 0.0).astype(BF16), preferred_element_type=F32)
-    place_one = first.astype(F32) * CAP + jnp.sum(jnp.where(one, before, 0.0), axis=0, keepdims=True)
-    place_two = second.astype(F32) * CAP + jnp.sum(jnp.where(two, before, 0.0), axis=0, keepdims=True)
+
+    def listed(route):
+        f = (((route >> 4) + zl) & 1) * 2 + ((route + core) & 1)
+        m = (y - ((route >> 1) & 7)) & 7
+        k = jnp.where(m <= 4, jnp.maximum(2 * m - 1, 0), 16 - 2 * m)
+        return ((7 - k) * 4 + f).astype(F32)
+
+    place_one = listed(first) * CAP + jnp.sum(jnp.where(one, before, 0.0), axis=0, keepdims=True)
+    place_two = listed(second) * CAP + jnp.sum(jnp.where(two, before, 0.0), axis=0, keepdims=True)
     places = lax.broadcasted_iota(jnp.int32, (EXPERTS * CAP, tokens), 0).astype(F32)
     at_one, at_two = places == place_one, places == place_two
     picks = (jnp.where(at_one, 1.0, 0.0) + jnp.where(at_two, 1.0, 0.0)).astype(BF16)
 
+    picked = jnp.dot(picks[: FAR * CAP], tz[zh], preferred_element_type=F32).astype(BF16)
+    out_far[...] = picked.reshape(FAR, CAP, width)
+
+    def dispatch_far(j, carry):
+        remote(
+            out_far.at[j], xs.at[j // PER, j % PER, zh], f_send, a_recv.at[j], (partner(j, -1), t)
+        ).start()
+        return carry
+
+    lax.fori_loop(0, FAR, dispatch_far, 0)
     for k in (0, 1, 3, 2):
         n = (zh + 4 - k) % RING
         if k:
-            arrived(tz.at[n], t_recv.at[k], over_z(1))
-        picked = jnp.dot(picks, tz[n], preferred_element_type=F32).astype(BF16)
-        outgoing[:, n] = picked.reshape(EXPERTS, CAP, width)
-
-    def dispatch(j, carry):
+            arrived(tz.at[n], t_recv.at[k], xu)
+        picked = jnp.dot(picks[FAR * CAP :], tz[n], preferred_element_type=F32).astype(BF16)
+        out_near[:, n] = picked.reshape(EXPERTS - FAR, CAP, width)
+
+    def dispatch_near(j, carry):
         @pl.when(j != HOME)
         def _():
-            d = partner(j, -1)
-            remote(outgoing.at[d], xs.at[j // PER, j % PER], a_send, a_recv.at[j], (d, t)).start()
-
-        return carry
-
-    lax.fori_loop(0, EXPERTS, dispatch, 0)
-    xs[HOME // PER, HOME % PER] = outgoing[e]
+            remote(
+                out_near.at[j - FAR], xs.at[j // PER, j % PER], a_send, a_recv.at[j], (partner(j, -1), t)
+            ).start()
+
+        return carry
+
+    lax.fori_loop(FAR, EXPERTS, dispatch_near, 0)
+    xs[HOME // PER, HOME % PER] = out_near[HOME - FAR]
+    for load in loads_in + loads_out:
+        load.start()
+
+    def spread(c, carry):
+        def wait(i, inner):
+            arrived(xs.at[0, 0, 0], a_recv.at[c * PER + i], xu)
+            return inner
+
+        lax.fori_loop(0, PER, wait, 0)
+        for k in (2, 1, 3):
+            own = xs.at[c, :, zh]
+            remote(own, own, q_send, q_recv.at[k - 1, c], over_z(k)).start()
+        return carry
+
+    lax.fori_loop(0, FAR_CHUNKS, spread, 0)
 
     arrived(w_in_relay.at[0], wi_recv.at[0], xu)
     remote(w_in_relay.at[0], w_in.at[0, x_dn], wi_send, wi_recv.at[6], xu).start()
     arrived(w_in_relay.at[1], wi_recv.at[1], xu)
     remote(w_in_relay.at[1], w_in.at[1, x_up], wi_send, wi_recv.at[7], xd).start()
+    remote(up_hbm.at[:, x_up], w_in.at[1, x], wi_send, wi_recv.at[4], xu).start()
+    remote(up_hbm.at[:, x_dn], w_in.at[1, x], wi_send, wi_recv.at[5], xd).start()
     for b in (0, 1):
         remote(down_hbm.at[:, columns(b, x_far)], w_out_relay.at[0, b], wo_send, wo_recv.at[0], xu).start()
         remote(
@@ -169,16 +202,24 @@
     arrived(w_in.at[1, x_far], wi_recv.at[7], xu)
 
     def project(c):
-        def wait(i, carry):
-            j = c * PER + i
-
-            @pl.when(j != HOME)
-            def _():
-                arrived(xs.at[0, 0], a_recv.at[j], xu)
-
-            return carry
-
-        lax.fori_loop(0, PER, wait, 0)
+        @pl.when(c < FAR_CHUNKS)
+        def _():
+            for k in (1, 3, 2):
+                arrived(xs.at[c, :, (zh + 4 - k) % RING], q_recv.at[k - 1, c], xu)
+
+        @pl.when(c >= FAR_CHUNKS)
+        def _():
+            def wait(i, carry):
+                j = c * PER + i
+
+                @pl.when(j != HOME)
+                def _():
+                    arrived(xs.at[0, 0], a_recv.at[j], xu)
+
+                return carry
+
+            lax.fori_loop(0, PER, wait, 0)
+
         for k in (2, 1, 3, 0):
             n = (x + k) % RING
             total = jnp.zeros((ROWS, 2 * block), F32)
@@ -226,13 +267,38 @@
             part = jnp.dot(hidden, w_out[b], preferred_element_type=F32).astype(BF16)
             ps[c, :, b] = part.reshape(PER, CAP, width)
 
+        @pl.when(c < FAR_CHUNKS)
+        def _():
+            for k in (2, 1, 3):
+                remote(
+                    ps.at[c, :, (zh + k) % RING], zs.at[k - 1, c], r_send, r_recv.at[k - 1, c], over_z(k)
+                ).start()
+
+        @pl.when(c >= FAR_CHUNKS)
+        def _():
+            def send(i, carry):
+                j = c * PER + i
+
+                @pl.when(j != HOME)
+                def _():
+                    remote(
+                        ps.at[c, i], back_near.at[j - FAR], b_send, b_recv.at[j], (partner(j, 1), t)
+                    ).start()
+
+                return carry
+
+            lax.fori_loop(0, PER, send, 0)
+
+    def settle(c):
+        total = ps[c, :, zh].astype(F32)
+        for k in (1, 3, 2):
+            arrived(zs.at[k - 1, c], r_recv.at[k - 1, c], xu)
+            total += zs[k - 1, c].astype(F32)
+        sums[c] = total.astype(BF16)
+
         def send(i, carry):
             j = c * PER + i
-
-            @pl.when(j != HOME)
-            def _():
-                remote(ps.at[c, i], back.at[e], b_send, b_recv.at[e], (partner(j, 1), t)).start()
-
+            remote(sums.at[c, i], back_far.at[j], s_send, b_recv.at[j], (partner(j, 1), t)).start()
             return carry
 
         lax.fori_loop(0, PER, send, 0)
@@ -254,30 +320,41 @@
         def _():
             expand(s - 2)
 
+        @pl.when((s >= 3) & (s < 3 + FAR_CHUNKS))
+        def _():
+            settle(s - 3)
+
         return carry
 
     lax.fori_loop(0, CHUNKS + 2, tick, 0)
-    back[e] = ps[HOME // PER, HOME % PER]
-
-    def collect(j, carry):
-        @pl.when(j != e)
-        def _():
-            arrived(back.at[0], b_recv.at[j], xu)
-
-        return carry
-
-    lax.fori_loop(0, EXPERTS, collect, 0)
+    back_near[HOME - FAR] = ps[HOME // PER, HOME % PER]
+
+    def collect_far(j, carry):
+        arrived(back_far.at[0], b_recv.at[j], xu)
+        return carry
+
+    def collect_near(j, carry):
+        @pl.when(j != HOME)
+        def _():
+            arrived(back_near.at[0], b_recv.at[j], xu)
+
+        return carry
+
+    def weigh(shares, returned):
+        both = jnp.dot(shares, returned.reshape(FAR * CAP, width), preferred_element_type=F32)
+        return both[:tokens] + both[tokens:]
 
     def combine(n):
-        returned = back[:, n].reshape(EXPERTS * CAP, width)
-        both = jnp.dot(share[...], returned, preferred_element_type=F32)
-        return both[:tokens] + both[tokens:]
-
+        return weigh(share[:, FAR * CAP :], back_near[:, n])
+
+    lax.fori_loop(0, FAR, collect_far, 0)
+    total = weigh(share[:, : FAR * CAP], back_far[...])
+    lax.fori_loop(FAR, EXPERTS, collect_near, 0)
     for k in (2, 1, 3):
         n = (zh + k) % RING
         cz[n] = combine(n).astype(BF16)
         remote(cz.at[n], zr.at[k - 1], z_send, z_recv.at[k - 1], over_z(k)).start()
-    total = combine(zh)
+    total += combine(zh)
     for k in (1, 3, 2):
         arrived(zr.at[k - 1], z_recv.at[k - 1], xu)
         total += zr[k - 1].astype(F32)
@@ -286,10 +363,15 @@
     sent(tz.at[pl.ds(0, 3)], t_send, xu)
     sent(w_in, wi_send, xu)
     sent(w_out, wo_send, xu)
-    sent(outgoing.at[pl.ds(0, EXPERTS - 1)], a_send, xu)
+    sent(out_far, f_send, xu)
+    sent(out_near.at[pl.ds(0, EXPERTS - FAR - 1)], a_send, xu)
+    some = (pl.ds(0, FAR_CHUNKS), slice(None), pl.ds(0, 3))
+    sent(xs.at[some], q_send, xu)
+    sent(ps.at[some], r_send, xu)
+    sent(back_far, s_send, xu)
     sent(gu_out.at[pl.ds(0, 3)], g_send, xu)
     sent(hs.at[pl.ds(0, 3)], h_send, xu)
-    sent(back.at[pl.ds(0, EXPERTS - 1)], b_send, xu)
+    sent(back_near.at[pl.ds(0, EXPERTS - FAR - 1)], b_send, xu)
     sent(cz.at[pl.ds(0, 3)], z_send, xu)
 
 
@@ -307,7 +389,8 @@
             vmem((RING, token_count, width), BF16),
             vmem((2, token_count), jnp.int32),
             vmem((2, token_count), F32),
-            vmem((EXPERTS, RING, CAP, width), BF16),
+            vmem((FAR, CAP, width), BF16),
+            vmem((EXPERTS - FAR, RING, CAP, width), BF16),
             vmem((CHUNKS, PER, RING, CAP, width), BF16),
             vmem((2,) + halves, BF16),
             vmem((2,) + halves[1:], BF16),
@@ -318,7 +401,10 @@
             vmem((RING - 1, CHUNKS, ROWS, 2 * block), BF16),
             vmem((RING, CHUNKS, ROWS, block), BF16),
             vmem((CHUNKS, PER, RING, CAP, width), BF16),
-            vmem((EXPERTS, RING, CAP, width), BF16),
+            vmem((RING - 1, FAR_CHUNKS, PER, CAP, width), BF16),
+            vmem((FAR_CHUNKS, PER, CAP, width), BF16),
+            vmem((FAR, CAP, width), BF16),
+            vmem((EXPERTS - FAR, RING, CAP, width), BF16),
             vmem((2 * token_count, EXPERTS * CAP), BF16),
             vmem((RING, token_count, width), BF16),
             vmem((RING - 1, token_count, width), BF16),
@@ -330,11 +416,17 @@
             dma,
             dma((6,)),
             dma,
+            dma,
             dma((EXPERTS,)),
             dma,
+            dma((RING - 1, FAR_CHUNKS)),
+            dma,
             dma((RING - 1, CHUNKS)),
             dma,
             dma((RING - 1, CHUNKS)),
+            dma,
+            dma((RING - 1, FAR_CHUNKS)),
+            dma,
             dma,
             dma((EXPERTS,)),
             dma,

time: 97.4 us -> 93.5 us (0.960)
  Pallas kernels: 95.7 us -> 91.8 us
    pallas_call x1, Pallas kernels: 95.7 us -> 91.8 us  [shards(): pl.pallas_call(layer, out_shape=jax.ShapeDtypeStruct((token_count, width)...]
where the time goes in v3:
time: 93.5 us; the launch traced here: 93.3 us
  Pallas kernels  91.8 us (98%)
  local copies, waits for them, and re-layouts  1.47 us (2%)
    pallas_call x1, Pallas kernels, shards(): pl.pallas_call(layer, out_shape=jax.ShapeDtypeStruct((token_count, width)...  91.8 us

profile of v3, /device:TPU:1, one launch (start us, length us, event | category | flops | bytes accessed | tf_op | source)
XLA Modules:
  0.0 93.3 jit_solution(14139528065909563735)
XLA Ops:
  0.0 91.8 %shard_map.64 = bf16[128,256]{1,0:T(8,128)(2,1)} custom-call(bf16[128,256]{1,0:T(8,128)(2,1)} %tok_hbm.1, s32[2,128]{1,0:T(2,128)} %bitcast.8, f32[2,128]{1,0:T(2,128)} %bitcast.9, bf16[4,4,256,128]{3,2,1,0:T(8,128)(2,1)} %bitcast.5, bf16[4,4,256,128]{3,2,1,0:T(8,128)(2,1)} %bitcast.6, bf16[128,4096]{1,0:T(8,128)(2,1)} %bitcast.7), custom_call_target="tpu_custom_call" | custom-call | tf_op jit(solution)/shard_map/pallas_call | solution.py:383
  91.9 1.5 %copy.8 = bf16[128,256]{1,0:T(8,128)(2,1)} copy(bf16[128,256]{1,0:T(8,128)(2,1)} %shard_map.64) | data formatting | bytes 131072

commit v4 on v2

v4 whole, which is shorter than its diff:
```python
import jax
import jax.numpy as jnp
from jax import lax
from jax.experimental import pallas as pl
from jax.experimental.pallas import tpu as pltpu
from jax.sharding import PartitionSpec as P

MESH = pl.DeviceIdType.MESH
F32, BF16 = jnp.float32, jnp.bfloat16
RING = 4
EXPERTS, CAP, CHUNKS = 32, 16, 4
PER = EXPERTS // CHUNKS
ROWS = PER * CAP
HOME = EXPERTS - 4
FAR_CHUNKS = 1
FAR = FAR_CHUNKS * PER


def remote(src, dst, send, recv, device):
    return pltpu.make_async_remote_copy(
        src_ref=src, dst_ref=dst, send_sem=send, recv_sem=recv, device_id=device, device_id_type=MESH
    )


def arrived(ref, sem, device):
    remote(ref, ref, sem, sem, device).wait_recv()


def sent(ref, sem, device):
    remote(ref, ref, sem, sem, device).wait_send()


def layer(
    tok_hbm, routes_hbm, gates_hbm, gate_hbm, up_hbm, down_hbm, out,
    tz, routes, gates, out_far, out_near, xs, w_in, w_out,
    gu_out, gu_own, gu_in, hs, ps, zs, sums, back, share,
    l_sem, t_send, t_recv, wi_send, wi_recv, wo_send, wo_recv, f_send, a_send, a_recv, q_send, q_recv,
    g_send, g_recv, h_send, h_recv, r_send, r_recv, s_send, s_recv,
):
    e, t = lax.axis_index("expert"), lax.axis_index("tensor")
    core, y, zl = e % 2, (e // 2) % 8, e // 16
    x, zh = t % RING, t // RING
    tokens, width = out.shape
    block = w_in.shape[-1]

    def over_x(k):
        return (e, zh * RING + (x + k) % RING)

    def over_z(k):
        return (e, ((zh + k) % RING) * RING + x)

    xu = over_x(1)

    layers, cores = (zl * 16, 16 - zl * 16), (core, 1 - core)

    def group(c, sign):
        found = []
        for dy in (4 - c, c - 3):
            rows = [((y + turn * sign * dy + 8) % 8) * 2 for turn in (1, -1)]
            found += [layers[f // 2] + rows[f % 2] + cores[f % 2] for f in range(4)]
        return found

    lists = [group(c, -1) for c in range(CHUNKS)]
    barrier = pltpu.get_barrier_semaphore()
    for k in (1, 2, 3):
        pl.semaphore_signal(barrier, inc=1, device_id=over_z(k), device_id_type=MESH)
        pl.semaphore_signal(barrier, inc=1, device_id=over_x(k), device_id_type=MESH)
    for j in range(EXPERTS):
        if j != HOME:
            pl.semaphore_signal(barrier, inc=1, device_id=(lists[j // PER][j % PER], t), device_id_type=MESH)

    smalls = [
        pltpu.make_async_copy(tok_hbm, tz.at[zh], l_sem.at[0]),
        pltpu.make_async_copy(routes_hbm, routes, l_sem.at[1]),
        pltpu.make_async_copy(gates_hbm, gates, l_sem.at[2]),
    ]
    wide = RING * width

    def columns(n):
        return pl.ds(pl.multiple_of(n * wide, wide), wide)

    loads = [
        pltpu.make_async_copy(gate_hbm.at[:, x], w_in.at[0, x], l_sem.at[3]),
        pltpu.make_async_copy(up_hbm.at[:, x], w_in.at[1, x], l_sem.at[4]),
        pltpu.make_async_copy(down_hbm.at[:, columns(zh)], w_out.at[zh], l_sem.at[5]),
    ]
    for load in smalls:
        load.start()
    for load in smalls:
        load.wait()
    pl.semaphore_wait(barrier, EXPERTS - 1 + 6)

    for k in (2, 1, 3):
        remote(tz.at[zh], tz.at[zh], t_send, t_recv.at[k], over_z(k)).start()
    for k in (2, 1, 3):
        n = (x + k) % RING
        remote(gate_hbm.at[:, n], w_in.at[0, x], wi_send, wi_recv.at[0, k - 1], over_x(k)).start()
        remote(up_hbm.at[:, n], w_in.at[1, x], wi_send, wi_recv.at[1, k - 1], over_x(k)).start()

    first, second = routes[0:1, :], routes[1:2, :]
    names = lax.broadcasted_iota(jnp.int32, (EXPERTS, tokens), 0)
    one, two = names == first, names == second
    count = (jnp.where(one, 1.0, 0.0) + jnp.where(two, 1.0, 0.0)).astype(BF16)
    earlier = lax.broadcasted_iota(jnp.int32, (tokens, tokens), 0) < lax.broadcasted_iota(
        jnp.int32, (tokens, tokens), 1
    )
    before = jnp.dot(count, jnp.where(earlier, 1.0, 0.0).astype(BF16), preferred_element_type=F32)

    def listed(route):
        f = (((route >> 4) + zl) & 1) * 2 + ((route + core) & 1)
        turn = 1 - 2 * ((route + core) & 1)
        m = ((y - ((route >> 1) & 7)) * turn) & 7
        k = jnp.where(m <= 4, jnp.maximum(2 * m - 1, 0), 16 - 2 * m)
        return ((7 - k) * 4 + f).astype(F32)

    place_one = listed(first) * CAP + jnp.sum(jnp.where(one, before, 0.0), axis=0, keepdims=True)
    place_two = listed(second) * CAP + jnp.sum(jnp.where(two, before, 0.0), axis=0, keepdims=True)
    places = lax.broadcasted_iota(jnp.int32, (EXPERTS * CAP, tokens), 0).astype(F32)
    at_one, at_two = places == place_one, places == place_two
    picks = (jnp.where(at_one, 1.0, 0.0) + jnp.where(at_two, 1.0, 0.0)).astype(BF16)

    picked = jnp.dot(picks[: FAR * CAP], tz[zh], preferred_element_type=F32).astype(BF16)
    out_far[...] = picked.reshape(FAR, CAP, width)

    for j in range(FAR):
        c, i = j // PER, j % PER
        remote(out_far.at[j], xs.at[c, i, zh], f_send, a_recv.at[c], (lists[c][i], t)).start()
    for k in (0, 1, 3, 2):
        n = (zh + 4 - k) % RING
        if k:
            arrived(tz.at[n], t_recv.at[k], xu)
        picked = jnp.dot(picks[FAR * CAP :], tz[n], preferred_element_type=F32).astype(BF16)
        out_near[:, n] = picked.reshape(EXPERTS - FAR, CAP, width)

    for j in range(FAR, EXPERTS):
        c, i = j // PER, j % PER
        if j != HOME:
            remote(out_near.at[j - FAR], xs.at[c, i], a_send, a_recv.at[c], (lists[c][i], t)).start()
    xs[HOME // PER, HOME % PER] = out_near[HOME - FAR]
    for k in (2, 1, 3):
        n = (zh + k) % RING
        remote(down_hbm.at[:, columns(n)], w_out.at[zh], wo_send, wo_recv.at[k - 1], over_z(k)).start()
    for load in loads:
        load.start()

    def spread(c, carry):
        arrived(xs.at[c, :, zh], a_recv.at[c], xu)
        for k in (2, 1, 3):
            own = xs.at[c, :, zh]
            remote(own, own, q_send, q_recv.at[k - 1, c], over_z(k)).start()
        return carry

    lax.fori_loop(0, FAR_CHUNKS, spread, 0)

    shared = jnp.where(at_one, gates[0:1, :], 0.0) + jnp.where(at_two, gates[1:2, :], 0.0)
    shared = shared.T
    coarse = shared.astype(BF16)
    share[0:tokens, :] = coarse
    share[tokens : 2 * tokens, :] = (shared - coarse.astype(F32)).astype(BF16)

    for load in loads:
        load.wait()
    for k in (1, 3, 2):
        for m in (0, 1):
            arrived(w_in.at[m, (x + 4 - k) % RING], wi_recv.at[m, k - 1], xu)

    def project(c):
        @pl.when(c < FAR_CHUNKS)
        def _():
            for k in (1, 3, 2):
                arrived(xs.at[c, :, (zh + 4 - k) % RING], q_recv.at[k - 1, c], xu)

        @pl.when((c >= FAR_CHUNKS) & (c < CHUNKS - 1))
        def _():
            arrived(xs.at[c], a_recv.at[c], xu)

        @pl.when(c == CHUNKS - 1)
        def _():
            arrived(xs.at[c, pl.ds(0, PER - 1)], a_recv.at[c], xu)

        for k in (2, 1, 3, 0):
            n = (x + k) % RING
            total = jnp.zeros((ROWS, 2 * block), F32)
            for b in range(RING):
                weights = jnp.concatenate([w_in[0, n, b], w_in[1, n, b]], axis=1)
                total += jnp.dot(xs[c, :, b].reshape(ROWS, width), weights, preferred_element_type=F32)
            if k:
                gu_out[n, c] = total.astype(BF16)
                remote(gu_out.at[n, c], gu_in.at[k - 1, c], g_send, g_recv.at[k - 1, c], over_x(k)).start()
            else:
                gu_own[c] = total

    def activate(c):
        total = gu_own[c]
        for k in (1, 3, 2):
            arrived(gu_in.at[k - 1, c], g_recv.at[k - 1, c], xu)
            total += gu_in[k - 1, c].astype(F32)
        gate, up = total[:, :block], total[:, block:]
        hs[zh, c] = (gate / (1.0 + jnp.exp(-gate)) * up).astype(BF16)
        for k in (2, 1, 3):
            remote(hs.at[zh, c], hs.at[zh, c], h_send, h_recv.at[k - 1, c], over_z(k)).start()

    def have_out():
        for k in (1, 3, 2):
            arrived(w_out.at[(zh + 4 - k) % RING], wo_recv.at[k - 1], xu)

    def expand(c):
        for k in (1, 3, 2):
            arrived(hs.at[(zh + 4 - k) % RING, c], h_recv.at[k - 1, c], xu)
        hidden = jnp.concatenate([hs[n, c] for n in range(RING)], axis=1)
        weights = w_out[...].reshape(RING * block, wide)
        for n in range(RING):
            part = jnp.dot(hidden, weights[:, n * width : (n + 1) * width], preferred_element_type=F32)
            ps[c, n] = part.astype(BF16)
        for k in (2, 1, 3):
            remote(
                ps.at[c, (x + k) % RING], zs.at[k - 1, c], r_send, r_recv.at[k - 1, c], over_x(k)
            ).start()

    def settle(c):
        total = ps[c, x].astype(F32)
        for k in (1, 3, 2):
            arrived(zs.at[k - 1, c], r_recv.at[k - 1, c], xu)
            total += zs[k - 1, c].astype(F32)
        sums[c] = total.astype(BF16).reshape(PER, CAP, width)
        sources = group(c, 1)
        for i in range(PER):

            def send(i=i):
                remote(sums.at[c, i], back.at[c * PER + i], s_send, s_recv, (sources[i], t)).start()

            pl.when(c < CHUNKS - 1)(send) if i == HOME % PER else send()

    def each(c, carry):
        project(c)
        return carry

    lax.fori_loop(0, CHUNKS, each, 0)

    def tick(s, carry):
        pl.when(s < CHUNKS)(lambda: activate(s))
        pl.when(s == 2)(have_out)
        pl.when((s >= 2) & (s < CHUNKS + 2))(lambda: expand(s - 2))
        pl.when(s >= 3)(lambda: settle(s - 3))
        return carry

    lax.fori_loop(0, CHUNKS + 3, tick, 0)
    back[HOME] = sums[HOME // PER, HOME % PER]
    arrived(back.at[pl.ds(0, EXPERTS - 1)], s_recv, xu)
    both = jnp.dot(share[...], back[...].reshape(EXPERTS * CAP, width), preferred_element_type=F32)
    out[...] = (both[:tokens] + both[tokens:]).astype(BF16)

    sent(tz.at[pl.ds(0, 3)], t_send, xu)
    sent(w_in.at[:, pl.ds(0, 3)], wi_send, xu)
    sent(w_out.at[pl.ds(0, 3)], wo_send, xu)
    sent(out_far, f_send, xu)
    sent(out_near.at[pl.ds(0, EXPERTS - FAR - 1)], a_send, xu)
    sent(xs.at[pl.ds(0, FAR_CHUNKS), :, pl.ds(0, 3)], q_send, xu)
    sent(gu_out.at[pl.ds(0, 3)], g_send, xu)
    sent(hs.at[pl.ds(0, 3)], h_send, xu)
    sent(ps.at[:, pl.ds(0, 3)], r_send, xu)
    sent(back.at[pl.ds(0, EXPERTS - 1)], s_send, xu)


def shards(tokens, routes, route_gates, gate_weight, up_weight, down_weight):
    token_count, width = tokens.shape
    depth, block = gate_weight.shape[1:]
    dma, vmem = pltpu.SemaphoreType.DMA, pltpu.VMEM
    halves = (RING, RING, width, block)
    return pl.pallas_call(
        layer,
        out_shape=jax.ShapeDtypeStruct((token_count, width), BF16),
        in_specs=[pl.BlockSpec(memory_space=pltpu.HBM)] * 6,
        out_specs=pl.BlockSpec(memory_space=vmem),
        scratch_shapes=[
            vmem((RING, token_count, width), BF16),
            vmem((2, token_count), jnp.int32),
            vmem((2, token_count), F32),
            vmem((FAR, CAP, width), BF16),
            vmem((EXPERTS - FAR, RING, CAP, width), BF16),
            vmem((CHUNKS, PER, RING, CAP, width), BF16),
            vmem((2,) + halves, BF16),
            vmem((RING, block, RING * width), BF16),
            vmem((RING, CHUNKS, ROWS, 2 * block), BF16),
            vmem((CHUNKS, ROWS, 2 * block), F32),
            vmem((RING - 1, CHUNKS, ROWS, 2 * block), BF16),
            vmem((RING, CHUNKS, ROWS, block), BF16),
            vmem((CHUNKS, RING, ROWS, width), BF16),
            vmem((RING - 1, CHUNKS, ROWS, width), BF16),
            vmem((CHUNKS, PER, CAP, width), BF16),
            vmem((EXPERTS, CAP, width), BF16),
            vmem((2 * token_count, EXPERTS * CAP), BF16),
            dma((6,)),
            dma,
            dma((RING,)),
            dma,
            dma((2, RING - 1)),
            dma,
            dma((RING - 1,)),
            dma,
            dma,
            dma((CHUNKS,)),
            dma,
            dma((RING - 1, FAR_CHUNKS)),
            dma,
            dma((RING - 1, CHUNKS)),
            dma,
            dma((RING - 1, CHUNKS)),
            dma,
            dma((RING - 1, CHUNKS)),
            dma,
            dma,
        ],
        compiler_params=pltpu.CompilerParams(
            collective_id=0, has_side_effects=True, vmem_limit_bytes=62 * 1024 * 1024
        ),
    )(
        tokens,
        routes.T,
        route_gates.T,
        gate_weight.reshape(halves),
        up_weight.reshape(halves),
        down_weight[0],
    )


def solution(mesh):
    return jax.shard_map(
        shards,
        mesh=mesh,
        in_specs=(
            P("expert", "tensor"),
            P("expert", None),
            P("expert", None),
            P("expert", None, "tensor"),
            P("expert", None, "tensor"),
            P("expert", "tensor", None),
        ),
        out_specs=P("expert", "tensor"),
        check_vma=False,
    )
```

time: 97.4 us -> 95.7 us (0.983)
  Pallas kernels: 95.7 us -> 94 us
    pallas_call x1, Pallas kernels: 95.7 us -> 94 us  [shards(): pl.pallas_call(layer, out_shape=jax.ShapeDtypeStruct((token_count, width)...]
where the time goes in v4:
time: 95.7 us; the launch traced here: 95.5 us
  Pallas kernels  94 us (98%)
  local copies, waits for them, and re-layouts  1.47 us (2%)
    pallas_call x1, Pallas kernels, shards(): pl.pallas_call(layer, out_shape=jax.ShapeDtypeStruct((token_count, width)...  94 us

profile of v4, /device:TPU:1, one launch (start us, length us, event | category | flops | bytes accessed | tf_op | source)
XLA Modules:
  0.0 95.5 jit_solution(785686355868916754)
XLA Ops:
  0.0 94.0 %shard_map.64 = bf16[128,256]{1,0:T(8,128)(2,1)} custom-call(bf16[128,256]{1,0:T(8,128)(2,1)} %tok_hbm.1, s32[2,128]{1,0:T(2,128)} %bitcast.8, f32[2,128]{1,0:T(2,128)} %bitcast.9, bf16[4,4,256,128]{3,2,1,0:T(8,128)(2,1)} %bitcast.5, bf16[4,4,256,128]{3,2,1,0:T(8,128)(2,1)} %bitcast.6, bf16[128,4096]{1,0:T(8,128)(2,1)} %bitcast.7), custom_call_target="tpu_custom_call" | custom-call | tf_op jit(solution)/shard_map/pallas_call | solution.py:270
  94.0 1.5 %copy.8 = bf16[128,256]{1,0:T(8,128)(2,1)} copy(bf16[128,256]{1,0:T(8,128)(2,1)} %shard_map.64) | data formatting | bytes 131072

commit v5 on v3

--- a/solution.py
+++ b/solution.py
@@ -12,8 +12,8 @@
 PER = EXPERTS // CHUNKS
 ROWS = PER * CAP
 HOME = EXPERTS - 4
-FAR = EXPERTS // 2
-FAR_CHUNKS = CHUNKS // 2
+FAR = EXPERTS // 4
+FAR_CHUNKS = 1
 
 
 def remote(src, dst, send, recv, device):
@@ -51,24 +51,23 @@
     def over_z(k):
         return (e, ((zh + k) % RING) * RING + x)
 
-    def partner(j, sign):
-        k, f = 7 - j // 4, j % 4
-        dy = (k % 2) * ((k + 1) // 2) - (1 - k % 2) * (k // 2)
-        return (((zl + f // 2) % 2) * 8 + (y + sign * dy + 8) % 8) * 2 + (core + f % 2) % 2
-
+    layers, cores = (zl * 16, 16 - zl * 16), (core, 1 - core)
+
+    def group(c, sign):
+        found = []
+        for dy in (4 - c, c - 3):
+            rows = [((y + turn * sign * dy + 8) % 8) * 2 for turn in (1, -1)]
+            found += [layers[f // 2] + rows[f % 2] + cores[f % 2] for f in range(4)]
+        return found
+
+    lists = [group(c, -1) for c in range(CHUNKS)]
     barrier = pltpu.get_barrier_semaphore()
-
-    def greet(j, carry):
-        @pl.when(j != HOME)
-        def _():
-            pl.semaphore_signal(barrier, inc=1, device_id=(partner(j, 1), t), device_id_type=MESH)
-
-        return carry
-
     for k in (1, 2, 3):
         pl.semaphore_signal(barrier, inc=1, device_id=over_z(k), device_id_type=MESH)
         pl.semaphore_signal(barrier, inc=1, device_id=over_x(k), device_id_type=MESH)
-    lax.fori_loop(0, EXPERTS, greet, 0)
+    for j in range(EXPERTS):
+        if j != HOME:
+            pl.semaphore_signal(barrier, inc=1, device_id=(lists[j // PER][j % PER], t), device_id_type=MESH)
 
     smalls = [
         pltpu.make_async_copy(tok_hbm, tz.at[zh], l_sem.at[0]),
@@ -113,7 +112,8 @@
 
     def listed(route):
         f = (((route >> 4) + zl) & 1) * 2 + ((route + core) & 1)
-        m = (y - ((route >> 1) & 7)) & 7
+        turn = 1 - 2 * ((route + core) & 1)
+        m = ((y - ((route >> 1) & 7)) * turn) & 7
         k = jnp.where(m <= 4, jnp.maximum(2 * m - 1, 0), 16 - 2 * m)
         return ((7 - k) * 4 + f).astype(F32)
 
@@ -126,13 +126,9 @@
     picked = jnp.dot(picks[: FAR * CAP], tz[zh], preferred_element_type=F32).astype(BF16)
     out_far[...] = picked.reshape(FAR, CAP, width)
 
-    def dispatch_far(j, carry):
-        remote(
-            out_far.at[j], xs.at[j // PER, j % PER, zh], f_send, a_recv.at[j], (partner(j, -1), t)
-        ).start()
-        return carry
-
-    lax.fori_loop(0, FAR, dispatch_far, 0)
+    for j in range(FAR):
+        c, i = j // PER, j % PER
+        remote(out_far.at[j], xs.at[c, i, zh], f_send, a_recv.at[c], (lists[c][i], t)).start()
     for k in (0, 1, 3, 2):
         n = (zh + 4 - k) % RING
         if k:
@@ -140,26 +136,16 @@
         picked = jnp.dot(picks[FAR * CAP :], tz[n], preferred_element_type=F32).astype(BF16)
         out_near[:, n] = picked.reshape(EXPERTS - FAR, CAP, width)
 
-    def dispatch_near(j, carry):
-        @pl.when(j != HOME)
-        def _():
-            remote(
-                out_near.at[j - FAR], xs.at[j // PER, j % PER], a_send, a_recv.at[j], (partner(j, -1), t)
-            ).start()
-
-        return carry
-
-    lax.fori_loop(FAR, EXPERTS, dispatch_near, 0)
+    for j in range(FAR, EXPERTS):
+        c, i = j // PER, j % PER
+        if j != HOME:
+            remote(out_near.at[j - FAR], xs.at[c, i], a_send, a_recv.at[c], (lists[c][i], t)).start()
     xs[HOME // PER, HOME % PER] = out_near[HOME - FAR]
     for load in loads_in + loads_out:
         load.start()
 
     def spread(c, carry):
-        def wait(i, inner):
-            arrived(xs.at[0, 0, 0], a_recv.at[c * PER + i], xu)
-            return inner
-
-        lax.fori_loop(0, PER, wait, 0)
+        arrived(xs.at[c, :, zh], a_recv.at[c], xu)
         for k in (2, 1, 3):
             own = xs.at[c, :, zh]
             remote(own, own, q_send, q_recv.at[k - 1, c], over_z(k)).start()
@@ -207,18 +193,13 @@
             for k in (1, 3, 2):
                 arrived(xs.at[c, :, (zh + 4 - k) % RING], q_recv.at[k - 1, c], xu)
 
-        @pl.when(c >= FAR_CHUNKS)
-        def _():
-            def wait(i, carry):
-                j = c * PER + i
-
-                @pl.when(j != HOME)
-                def _():
-                    arrived(xs.at[0, 0], a_recv.at[j], xu)
-
-                return carry
-
-            lax.fori_loop(0, PER, wait, 0)
+        @pl.when((c >= FAR_CHUNKS) & (c < CHUNKS - 1))
+        def _():
+            arrived(xs.at[c], a_recv.at[c], xu)
+
+        @pl.when(c == CHUNKS - 1)
+        def _():
+            arrived(xs.at[c, pl.ds(0, PER - 1)], a_recv.at[c], xu)
 
         for k in (2, 1, 3, 0):
             n = (x + k) % RING
@@ -276,18 +257,16 @@
 
         @pl.when(c >= FAR_CHUNKS)
         def _():
-            def send(i, carry):
-                j = c * PER + i
-
-                @pl.when(j != HOME)
-                def _():
+            sources = group(c, 1)
+            for i in range(PER):
+
+                def send(i=i):
                     remote(
-                        ps.at[c, i], back_near.at[j - FAR], b_send, b_recv.at[j], (partner(j, 1), t)
+                        ps.at[c, i], back_near.at[(c - FAR_CHUNKS) * PER + i], b_send, b_recv.at[1],
+                        (sources[i], t),
                     ).start()
 
-                return carry
-
-            lax.fori_loop(0, PER, send, 0)
+                pl.when(c < CHUNKS - 1)(send) if i == HOME % PER else send()
 
     def settle(c):
         total = ps[c, :, zh].astype(F32)
@@ -296,12 +275,11 @@
             total += zs[k - 1, c].astype(F32)
         sums[c] = total.astype(BF16)
 
-        def send(i, carry):
-            j = c * PER + i
-            remote(sums.at[c, i], back_far.at[j], s_send, b_recv.at[j], (partner(j, 1), t)).start()
-            return carry
-
-        lax.fori_loop(0, PER, send, 0)
+        sources = group(c, 1)
+        for i in range(PER):
+            remote(
+                sums.at[c, i], back_far.at[c * PER + i], s_send, b_recv.at[0], (sources[i], t)
+            ).start()
 
     def tick(s, carry):
         @pl.when(s < CHUNKS)
@@ -329,27 +307,16 @@
     lax.fori_loop(0, CHUNKS + 2, tick, 0)
     back_near[HOME - FAR] = ps[HOME // PER, HOME % PER]
 
-    def collect_far(j, carry):
-        arrived(back_far.at[0], b_recv.at[j], xu)
-        return carry
-
-    def collect_near(j, carry):
-        @pl.when(j != HOME)
-        def _():
-            arrived(back_near.at[0], b_recv.at[j], xu)
-
-        return carry
-
     def weigh(shares, returned):
-        both = jnp.dot(shares, returned.reshape(FAR * CAP, width), preferred_element_type=F32)
+        both = jnp.dot(shares, returned.reshape(returned.shape[0] * CAP, width), preferred_element_type=F32)
         return both[:tokens] + both[tokens:]
 
     def combine(n):
         return weigh(share[:, FAR * CAP :], back_near[:, n])
 
-    lax.fori_loop(0, FAR, collect_far, 0)
+    arrived(back_far, b_recv.at[0], xu)
     total = weigh(share[:, : FAR * CAP], back_far[...])
-    lax.fori_loop(FAR, EXPERTS, collect_near, 0)
+    arrived(back_near.at[pl.ds(0, EXPERTS - FAR - 1)], b_recv.at[1], xu)
     for k in (2, 1, 3):
         n = (zh + k) % RING
         cz[n] = combine(n).astype(BF16)
@@ -417,7 +384,7 @@
             dma((6,)),
             dma,
             dma,
-            dma((EXPERTS,)),
+            dma((CHUNKS,)),
             dma,
             dma((RING - 1, FAR_CHUNKS)),
             dma,
@@ -428,7 +395,7 @@
             dma((RING - 1, FAR_CHUNKS)),
             dma,
             dma,
-            dma((EXPERTS,)),
+            dma((2,)),
             dma,
             dma((RING - 1,)),
         ],

time: 93.5 us -> 92 us (0.984)
  Pallas kernels: 91.8 us -> 90.3 us
    pallas_call x1, Pallas kernels: 91.8 us -> 90.3 us  [shards(): pl.pallas_call(layer, out_shape=jax.ShapeDtypeStruct((token_count, width)...]
where the time goes in v5:
time: 92 us; the launch traced here: 91.8 us
  Pallas kernels  90.3 us (98%)
  local copies, waits for them, and re-layouts  1.47 us (2%)
    pallas_call x1, Pallas kernels, shards(): pl.pallas_call(layer, out_shape=jax.ShapeDtypeStruct((token_count, width)...  90.3 us

profile of v5, /device:TPU:1, one launch (start us, length us, event | category | flops | bytes accessed | tf_op | source)
XLA Modules:
  0.0 91.8 jit_solution(4590743568216537543)
XLA Ops:
  0.0 90.3 %shard_map.64 = bf16[128,256]{1,0:T(8,128)(2,1)} custom-call(bf16[128,256]{1,0:T(8,128)(2,1)} %tok_hbm.1, s32[2,128]{1,0:T(2,128)} %bitcast.8, f32[2,128]{1,0:T(2,128)} %bitcast.9, bf16[4,4,256,128]{3,2,1,0:T(8,128)(2,1)} %bitcast.5, bf16[4,4,256,128]{3,2,1,0:T(8,128)(2,1)} %bitcast.6, bf16[128,4096]{1,0:T(8,128)(2,1)} %bitcast.7), custom_call_target="tpu_custom_call" | custom-call | tf_op jit(solution)/shard_map/pallas_call | solution.py:350
  90.3 1.5 %copy.8 = bf16[128,256]{1,0:T(8,128)(2,1)} copy(bf16[128,256]{1,0:T(8,128)(2,1)} %shard_map.64) | data formatting | bytes 131072

commit v6 on v5

--- a/solution.py
+++ b/solution.py
@@ -61,6 +61,13 @@
         return found
 
     lists = [group(c, -1) for c in range(CHUNKS)]
+    smalls = [
+        pltpu.make_async_copy(tok_hbm, tz.at[zh], l_sem.at[0]),
+        pltpu.make_async_copy(routes_hbm, routes, l_sem.at[1]),
+        pltpu.make_async_copy(gates_hbm, gates, l_sem.at[2]),
+    ]
+    for load in smalls:
+        load.start()
     barrier = pltpu.get_barrier_semaphore()
     for k in (1, 2, 3):
         pl.semaphore_signal(barrier, inc=1, device_id=over_z(k), device_id_type=MESH)
@@ -69,11 +76,6 @@
         if j != HOME:
             pl.semaphore_signal(barrier, inc=1, device_id=(lists[j // PER][j % PER], t), device_id_type=MESH)
 
-    smalls = [
-        pltpu.make_async_copy(tok_hbm, tz.at[zh], l_sem.at[0]),
-        pltpu.make_async_copy(routes_hbm, routes, l_sem.at[1]),
-        pltpu.make_async_copy(gates_hbm, gates, l_sem.at[2]),
-    ]
     mine = pl.ds(pl.multiple_of(x * block, block), block)
     loads_in = [
         pltpu.make_async_copy(gate_hbm.at[:, x], w_in.at[0, x], l_sem.at[3]),
@@ -87,11 +89,9 @@
         pltpu.make_async_copy(down_hbm.at[:, columns(b, x)], w_out.at[b, mine], l_sem.at[5 + b])
         for b in range(RING)
     ]
-    for load in smalls:
-        load.start()
+    pl.semaphore_wait(barrier, EXPERTS - 1 + 6)
     for load in smalls:
         load.wait()
-    pl.semaphore_wait(barrier, EXPERTS - 1 + 6)
 
     for k in (2, 1, 3):
         remote(tz.at[zh], tz.at[zh], t_send, t_recv.at[k], over_z(k)).start()

time: 92 us -> 92 us (level)
  no operation moved by 1% of the time
where the time goes in v6:
time: 92 us; the launch traced here: 91.8 us
  Pallas kernels  90.3 us (98%)
  local copies, waits for them, and re-layouts  1.47 us (2%)
    pallas_call x1, Pallas kernels, shards(): pl.pallas_call(layer, out_shape=jax.ShapeDtypeStruct((token_count, width)...  90.3 us

profile of v6, /device:TPU:1, one launch (start us, length us, event | category | flops | bytes accessed | tf_op | source)
XLA Modules:
  0.0 91.8 jit_solution(4316388048182273850)
XLA Ops:
  0.0 90.3 %shard_map.64 = bf16[128,256]{1,0:T(8,128)(2,1)} custom-call(bf16[128,256]{1,0:T(8,128)(2,1)} %tok_hbm.1, s32[2,128]{1,0:T(2,128)} %bitcast.8, f32[2,128]{1,0:T(2,128)} %bitcast.9, bf16[4,4,256,128]{3,2,1,0:T(8,128)(2,1)} %bitcast.5, bf16[4,4,256,128]{3,2,1,0:T(8,128)(2,1)} %bitcast.6, bf16[128,4096]{1,0:T(8,128)(2,1)} %bitcast.7), custom_call_target="tpu_custom_call" | custom-call | tf_op jit(solution)/shard_map/pallas_call | solution.py:350
  90.3 1.5 %copy.8 = bf16[128,256]{1,0:T(8,128)(2,1)} copy(bf16[128,256]{1,0:T(8,128)(2,1)} %shard_map.64) | data formatting | bytes 131072
